TPU v7x, 128 devices: a whole 4x4x4 slice. The times are simulated.
128 devices in a mesh: dp: 32 (over z_lo, x, y), tensor: 4 (over z_hi, core).
Axes of the slice: x: 4, y: 4, z: 4 (z_hi: 2, z_lo: 2; z = z_hi * 2 + z_lo), core: 2. Of those that a mesh axis runs over, the one named last changes fastest.
Arguments:
- hidden: bfloat16 [64, 512, 5120], P('dp'), may hold values from -5 to 5
- query_projection_matrix: bfloat16 [5120, 2560], P('dp', 'tensor'), may hold values from -0.5 to 0.5
- key_projection_matrix: bfloat16 [5120, 2560], P('dp', 'tensor'), may hold values from -0.5 to 0.5
- value_projection_matrix: bfloat16 [5120, 2560], P('dp', 'tensor'), may hold values from -0.078125 to 0.078125
- adapter_down_maps: bfloat16 [2, 8, 5120], replicated, may hold values from -0.078125 to 0.078125
- adapter_up_maps: bfloat16 [2, 8, 2560], P(None, None, 'tensor'), may hold values from -1 to 1
- cotangent: bfloat16 [64, 512, 2560], P('dp', None, 'tensor'), may hold values from -6 to 6
- lengths: int32 [64], P('dp'), may hold values from 1 to 512, 16640 in all
- random_signs_down: bfloat16 [2, 8, 5120, 4096], P(None, None, ('dp', 'tensor')), may hold values from -4 to 4
- random_signs_up: bfloat16 [2, 8, 20, 128, 4096], P(None, None, 'tensor', 'dp'), may hold values from -4 to 4
Outputs:
- features: float32 [64, 4096], P('dp', 'tensor')
Inputs may be any that keep to these rules, and one draw needn't show every extreme that they name: `lengths`: positions at or beyond an example's length are padding.
All inputs are finite; a program needn't handle non-finite values. No bound on the sum of `lengths` on one device may be relied on, other than what follows from the above.
Results may differ from a plain program's by a relative error of at most 0.025.
Values may be sent and summed in bfloat16 or wider, within the bound.
A program may use at most 128 MiB of HBM per device.

v0:
```python
import jax
import jax.numpy as jnp
from jax import lax
from jax.sharding import PartitionSpec as P

HEAD_DIM = 128
ADAPTER_RANK = 8
FEAT = 4096
adapter_scale = 2.0
rope_base = 10000.0
norm_eps = 1e-05
masked_score = -1e30


def rope_tables(seq_len, head_width):
    half_width = head_width // 2
    frequency = rope_base ** (-2.0 * jnp.arange(half_width, dtype=jnp.float32) / head_width)
    angles = jnp.arange(seq_len, dtype=jnp.float32)[:, None] * frequency[None, :]
    rotary_cosines = jnp.concatenate([jnp.cos(angles), jnp.cos(angles)], axis=1)
    rotary_sines = jnp.concatenate([jnp.sin(angles), jnp.sin(angles)], axis=1)
    return (rotary_cosines, rotary_sines)


def apply_rotary(tensor_in, rotary_cosines, rotary_sines):
    half_width = tensor_in.shape[-1] // 2
    turned = jnp.concatenate([-tensor_in[..., half_width:], tensor_in[..., :half_width]], axis=-1)
    return tensor_in * rotary_cosines[:, None, :] + turned * rotary_sines[:, None, :]


def unrotate(gradient, rotary_cosines, rotary_sines):
    half_width = gradient.shape[-1] // 2
    scaled = gradient * rotary_sines[:, None, :]
    rotated_back = jnp.concatenate([scaled[..., half_width:], -scaled[..., :half_width]], axis=-1)
    return gradient * rotary_cosines[:, None, :] + rotated_back


def attention_grads(example):
    query_per_head, key_heads, value_per_head, grad_out, seq_length = example
    seq_len = query_per_head.shape[0]
    inv_root = query_per_head.shape[-1] ** (-0.5)
    scores = (
        jnp.einsum("qhc,khc->hqk", query_per_head, key_heads, preferred_element_type=jnp.float32)
        * inv_root
    )
    query_pos = jnp.arange(seq_len, dtype=jnp.int32)[:, None]
    key_pos = jnp.arange(seq_len, dtype=jnp.int32)[None, :]
    allowed = (key_pos <= query_pos) & (key_pos < seq_length)
    scores = jnp.where(allowed[None], scores, masked_score)
    row_max = jnp.max(scores, axis=-1, keepdims=True)
    expon = jnp.exp(scores - row_max)
    attention = expon / jnp.sum(expon, axis=-1, keepdims=True)
    attention_low = attention.astype(jnp.bfloat16)
    grad_values = jnp.einsum(
        "hqk,qhc->khc", attention_low, grad_out, preferred_element_type=jnp.float32
    )
    grad_attention = jnp.einsum(
        "qhc,khc->hqk", grad_out, value_per_head, preferred_element_type=jnp.float32
    )
    inner_sum = jnp.sum(attention * grad_attention, axis=-1, keepdims=True)
    grad_scores = (attention * (grad_attention - inner_sum)).astype(jnp.bfloat16)
    grad_query = (
        jnp.einsum("hqk,khc->qhc", grad_scores, key_heads, preferred_element_type=jnp.float32)
        * inv_root
    )
    return (grad_query, grad_values)


def body(
    hidden,
    query_projection_matrix,
    key_projection_matrix,
    value_projection_matrix,
    adapter_down_maps,
    adapter_up_maps,
    cotangent,
    lengths,
    random_signs_down,
    random_signs_up,
):
    seq_count, seq_len, model_width = hidden.shape
    local_cols = query_projection_matrix.shape[1]
    heads_local = local_cols // HEAD_DIM
    token_matrix = hidden.reshape(seq_count * seq_len, model_width)

    def add_rows(weight_piece):
        return jnp.dot(token_matrix, weight_piece, preferred_element_type=jnp.float32)

    plain_query = add_rows(lax.all_gather(query_projection_matrix, "dp", axis=0, tiled=True))
    base_key = add_rows(lax.all_gather(key_projection_matrix, "dp", axis=0, tiled=True))
    plain_value = add_rows(lax.all_gather(value_projection_matrix, "dp", axis=0, tiled=True))
    rotary_cosines, rotary_sines = rope_tables(seq_len, HEAD_DIM)
    inner_hidden = jnp.einsum(
        "no,wio->nwi", token_matrix, adapter_down_maps, preferred_element_type=jnp.float32
    ).astype(jnp.bfloat16)
    raised_features = jnp.einsum(
        "kdg,dgj->kdj", inner_hidden, adapter_up_maps, preferred_element_type=jnp.float32
    )
    head_layout = (seq_count, seq_len, heads_local, HEAD_DIM)
    query_per_head = apply_rotary(
        (plain_query + adapter_scale * raised_features[:, 0]).reshape(head_layout),
        rotary_cosines,
        rotary_sines,
    ).astype(jnp.bfloat16)
    key_heads = apply_rotary(base_key.reshape(head_layout), rotary_cosines, rotary_sines).astype(
        jnp.bfloat16
    )
    value_per_head = (
        (plain_value + adapter_scale * raised_features[:, 1])
        .astype(jnp.bfloat16)
        .reshape(head_layout)
    )
    valid = jnp.arange(seq_len, dtype=jnp.int32)[None, :] < lengths[:, None]
    masked_out = jnp.where(valid[:, :, None], cotangent, jnp.zeros_like(cotangent)).reshape(
        head_layout
    )
    grad_query, grad_values = lax.map(
        attention_grads, (query_per_head, key_heads, value_per_head, masked_out, lengths)
    )
    grad_query = (
        unrotate(grad_query, rotary_cosines, rotary_sines)
        .astype(jnp.bfloat16)
        .reshape(seq_count, seq_len, local_cols)
    )
    grad_values = grad_values.astype(jnp.bfloat16).reshape(seq_count, seq_len, local_cols)
    per_head_gradient = jnp.stack([grad_query, grad_values], axis=2)
    branch_portion = jnp.einsum(
        "liov,ohv->lioh", per_head_gradient, adapter_up_maps, preferred_element_type=jnp.float32
    )
    adapter_branch = lax.psum(branch_portion, "tensor").astype(jnp.bfloat16)
    middle_seq = inner_hidden.reshape(seq_count, seq_len, 2, ADAPTER_RANK)
    up_map_gradient = adapter_scale * jnp.einsum(
        "esar,esac->earc", middle_seq, per_head_gradient, preferred_element_type=jnp.float32
    )
    parts_dp = lax.axis_size("dp")
    parts_tensor = lax.axis_size("tensor")
    row_block = model_width // (parts_dp * parts_tensor)
    hidden_blocks = hidden.reshape(seq_count, seq_len, parts_dp, parts_tensor, row_block)
    local_column_range = lax.dynamic_index_in_dim(
        hidden_blocks, lax.axis_index("tensor"), axis=3, keepdims=False
    )
    down_map_local = adapter_scale * jnp.einsum(
        "ykzu,ykhc->yhzuc", adapter_branch, local_column_range, preferred_element_type=jnp.float32
    )
    down_map_local = down_map_local.reshape(seq_count, parts_dp, 1, 2 * ADAPTER_RANK * row_block)
    slice_len = HEAD_DIM // parts_dp
    up_blocks = up_map_gradient.reshape(
        seq_count, 2, ADAPTER_RANK, heads_local, parts_dp, slice_len
    )
    up_blocks = up_blocks.transpose(0, 4, 1, 2, 3, 5).reshape(
        seq_count, parts_dp, 1, 2 * ADAPTER_RANK * heads_local * slice_len
    )
    packed = jnp.concatenate([down_map_local, up_blocks], axis=3).astype(jnp.bfloat16)
    routed = lax.all_to_all(packed, "dp", split_axis=1, concat_axis=0, tiled=True)
    gathered = routed.reshape(routed.shape[0], routed.shape[3])
    down_count = down_map_local.shape[3]
    down_table = random_signs_down.reshape(down_count, random_signs_down.shape[-1])
    up_table = random_signs_up.reshape(gathered.shape[1] - down_count, random_signs_up.shape[-1])
    own_rows = lax.psum_scatter(
        (
            jnp.dot(gathered[:, :down_count], down_table, preferred_element_type=jnp.float32)
            + jnp.dot(gathered[:, down_count:], up_table, preferred_element_type=jnp.float32)
        ).astype(jnp.bfloat16),
        "dp",
        scatter_dimension=0,
        tiled=True,
    )
    features_local = lax.psum_scatter(own_rows, "tensor", scatter_dimension=1, tiled=True).astype(
        jnp.float32
    )
    squares = lax.psum(jnp.sum(features_local * features_local, axis=1), "tensor")
    return features_local * lax.rsqrt(squares / FEAT + norm_eps)[:, None]


def solution(mesh):
    return jax.shard_map(
        body,
        mesh=mesh,
        in_specs=(
            P("dp", None, None),
            P("dp", "tensor"),
            P("dp", "tensor"),
            P("dp", "tensor"),
            P(),
            P(None, None, "tensor"),
            P("dp", None, "tensor"),
            P("dp"),
            P(None, None, ("dp", "tensor"), None),
            P(None, None, "tensor", "dp", None),
        ),
        out_specs=P("dp", "tensor"),
        check_vma=False,
    )
```

profile of v0, /device:TPU:1, one launch (start us, length us, event | category | flops | bytes accessed | tf_op | source)
XLA Modules:
  0.0 960.9 jit_solution(16384661594422788543)
XLA Ops:
  6.5 0.7 all-gather.6.cloned.1.call-update
  7.3 0.7 all-gather.4.cloned.1.call-update
  8.1 0.7 all-gather.8.cloned.1.call-update
  8.8 1.6 copy.57
  10.4 13.8 %copy.51 = bf16[2,512,5120]{1,2,0:T(8,128)(2,1)} copy(bf16[2,512,5120]{2,1,0:T(8,128)(2,1)} %param.12) | data formatting | bytes 20971520 | tf_op args[0]
  24.2 0.5 fusion.70
  24.9 1.2 broadcast_select_fusion
  26.1 6.8 convolution_convert_fusion
  32.9 0.6 copy-done.12
  33.5 3.2 convolution_bitcast_fusion
  36.7 117.4 %all-gather.6.cloned.1.call-done = bf16[5120,640]{1,0:T(8,128)(2,1)} async-done(((bf16[160,640]{1,0:T(8,128)(2,1)}), bf16[5120,640]{1,0:T(8,128)(2,1)}) %all-gather.6.cloned.1.call-update) | async-done | bytes 6553616 | tf_op jit(solution)/shard_map/all_gather | solution.py:88
  154.2 13.3 %fusion.46 = f32[1024,640]{1,0:T(8,128)S(1)} fusion(f32[1024,2,640]{2,0,1:T(8,128)} %convolution_bitcast_fusion, bf16[1024,5120]{1,0:T(8,128)(2,1)} %bitcast.136, bf16[5120,640]{1,0:T(8,128)(2,1)} %all-gather.6.cloned.1.call-done), kind=kOutput, calls=%fused_computation.52 | convolution fusion | flops 6712197120 | bytes 22282240 | tf_op jit(solution)/shard_map/dot_general | solution.py:86
  167.5 2.3 reshape.164
  169.8 3.3 copy.54
  173.1 145.5 %all-gather.4.cloned.1.call-done = bf16[5120,640]{1,0:T(8,128)(2,1)} async-done(((bf16[160,640]{1,0:T(8,128)(2,1)}), bf16[5120,640]{1,0:T(8,128)(2,1)}) %all-gather.4.cloned.1.call-update) | async-done | bytes 6553616 | tf_op jit(solution)/shard_map/all_gather | solution.py:89
  318.6 9.6 copy.52
  328.1 1.9 slice_negate_fusion.1
  330.1 11.9 %fusion.39 = f32[2,512,5,128]{1,3,2,0:T(8,128)S(1)} fusion(bf16[5,128,5120,1]{2,1,0,3:T(8,128)(2,1)} %bitcast.140, bf16[2,512,5120]{2,1,0:T(8,128)(2,1)} %param.12), kind=kOutput, calls=%fused_computation.42 | convolution fusion | flops 6710886400 | bytes 19660800 | tf_op jit(solution)/shard_map/dot_general | solution.py:86
  341.9 1.5 copy-done.3
  343.4 1.8 slice_negate_fusion.2
  345.2 137.9 %all-gather.8.cloned.1.call-done = bf16[5120,640]{1,0:T(8,128)(2,1)} async-done(((bf16[160,640]{1,0:T(8,128)(2,1)}), bf16[5120,640]{1,0:T(8,128)(2,1)}) %all-gather.8.cloned.1.call-update) | async-done | bytes 6553616 | tf_op jit(solution)/shard_map/all_gather | solution.py:90
  483.1 14.2 %fusion.44 = bf16[1024,640]{1,0:T(8,128)(2,1)} fusion(f32[1024,2,640]{2,0,1:T(8,128)} %convolution_bitcast_fusion, bf16[1024,5120]{1,0:T(8,128)(2,1)} %bitcast.137, bf16[5120,640]{1,0:T(8,128)(2,1)} %all-gather.8.cloned.1.call-done), kind=kOutput, calls=%fused_computation.49 | convolution fusion | flops 6712852480 | bytes 20971520 | tf_op jit(solution)/shard_map/dot_general | solution.py:86
  497.3 4.1 reshape.160
  501.4 3.1 copy.62
  504.4 5.5 fusion.50
  509.9 22.3 %while.12 = (s32[]{:T(128)}, f32[2,512,5,128]{1,3,2,0:T(8,128)}, bf16[2,512,5,128]{1,3,2,0:T(8,128)(2,1)}, bf16[2,512,5,128]{1,3,2,0:T(8,128)(2,1)}, s32[2]{0:T(...) while((s32[]{:T(128)}, f32[2,512,5,128]{1,3,2,0:T(8,128)}, ...), condition=%wide.region_4.5_spmd, body=%wide.region_0.4_spmd.sunk | while | flops 1362688512 | bytes 75326712 | solution.py:116
  509.9 2.2 fusion.110
  512.1 0.6 dynamic_slice.73
  512.7 0.6 iota_compare_fusion.4
  513.5 2.5 fusion.112
  516.1 1.0 fusion.114
  517.4 0.9 multiply_reduce_fusion.2
  518.2 0.6 copy-done.2
  518.9 2.2 fusion.113
  521.1 2.2 fusion.110
  523.2 0.6 dynamic_slice.73
  523.8 0.6 iota_compare_fusion.4
  524.6 2.5 fusion.112
  527.2 1.0 fusion.114
  528.5 0.8 multiply_reduce_fusion.2
  529.4 0.6 copy-done.2
  530.0 2.2 fusion.113
  532.2 2.1 broadcast_multiply_fusion
  534.6 2.5 fusion.51
  537.1 1.5 copy.63
  538.6 1.4 copy.64
  540.0 2.1 fusion.67
  542.1 34.5 %psum.14 = bf16[2,512,2,8]{1,3,2,0:T(8,128)(2,1)S(1)} all-reduce(f32[2,512,2,8]{1,3,2,0:T(8,128)S(1)} %fusion.67), channel_id=1, replica_groups=mesh['dp'=32,'tensor'=4] {'tensor'}, use_global_device_ids=true, to_apply=%region_5.6 | all-reduce | flops 16384 | bytes 98304 | tf_op jit(solution)/shard_map/psum | solution.py:129
  576.6 3.3 fusion.63
  580.3 0.5 fusion.68
  581.6 0.8 pad_maximum_fusion.11
  582.4 6.6 all-to-all-start
  589.1 3.5 reshape.153
  592.6 3.8 all-to-all-done
  596.6 3.6 fusion.71
  600.1 1.5 fusion.41
  601.7 0.6 dynamic-slice
  602.9 286.6 %all-reduce.3.cloned.1.call-done = bf16[64,4096]{1,0:T(8,128)(2,1)} async-done(((bf16[64,4096]{1,0:T(8,128)(2,1)}), bf16[64,4096]{1,0:T(8,128)(2,1)}) %all-reduce.3.cloned.1.call-update) | async-done | bytes 524304
  889.5 0.9 constant_dynamic-slice_fusion
  890.4 1.4 copy.79
  891.8 53.3 %reduce-scatter.4.cloned.1.call-done = bf16[1024,2]{1,0:T(8,128)(2,1)} async-done(((bf16[4096,2]{1,0:T(8,128)(2,1)}), bf16[1024,2]{1,0:T(8,128)(2,1)}) %reduce-scatter.4.cloned.1.call-update) | async-done | bytes 4112
  945.1 1.1 copy.80
  946.3 7.4 psum.15
  953.7 0.7 convert_multiply_fusion
  (65 shorter events, 3.0 us)
Async XLA Ops:
  6.5 19.5 %copy-start = (bf16[2,8,5120]{2,1,0:T(8,128)(2,1)S(1)}, bf16[2,8,5120]{2,1,0:T(8,128)(2,1)}, u32[]{:S(2)}) copy-start(bf16[2,8,5120]{2,1,0:T(8,128)(2,1)} %param.16) | copy-start | bytes 491524
  6.5 147.6 %all-gather.6.cloned.1.call-start = ((), (), s32[]{:S(2)}) async-start(), calls=%async_computation.3 | async-start | bytes 6758400 | tf_op jit(solution)/shard_map/all_gather | solution.py:88
  7.3 311.3 %all-gather.4.cloned.1.call-start = ((), (), s32[]{:S(2)}) async-start(), calls=%async_computation.2 | async-start | bytes 6758400 | tf_op jit(solution)/shard_map/all_gather | solution.py:89
  8.0 475.1 %all-gather.8.cloned.1.call-start = ((), (), s32[]{:S(2)}) async-start(), calls=%async_computation.4 | async-start | bytes 6758400 | tf_op jit(solution)/shard_map/all_gather | solution.py:90
  10.4 14.5 %copy-start.16 = (s32[2]{0:T(128)S(1)}, s32[2]{0:T(128)}, u32[]{:S(2)}) copy-start(s32[2]{0:T(128)} %param.19) | copy-start | bytes 28
  26.1 7.5 copy-start.14
  32.9 0.6 copy-start.12
  341.9 1.5 copy-start.3
  501.4 3.1 copy-start.4
  513.5 2.6 copy-start.5
  513.5 2.6 copy-start.11
  516.1 1.3 copy-start.8
  517.1 1.2 copy-start.6
  517.4 1.5 copy-start.2
  524.6 2.6 copy-start.5
  524.6 2.6 copy-start.11
  527.2 1.3 copy-start.8
  528.2 1.2 copy-start.6
  528.5 1.5 copy-start.2
  537.1 1.5 copy-start.7
  537.1 2.9 copy-start.15
  538.6 1.4 copy-start.9
  542.1 38.1 %copy-start.10 = (bf16[2,512,1,640]{3,1,2,0:T(8,128)(2,1)S(1)}, bf16[2,512,1,640]{3,1,2,0:T(8,128)(2,1)}, u32[]{:S(2)}) copy-start(bf16[2,512,1,640]{3,1,2,0:T(8,128)(2,1)} %copy.64) | copy-start | bytes 3932164
  542.1 38.1 %copy-start.13 = (bf16[1024,2,8]{0,2,1:T(8,128)(2,1)S(1)}, bf16[1024,2,8]{0,2,1:T(8,128)(2,1)}, u32[]{:S(2)}) copy-start(bf16[1024,2,8]{0,2,1:T(8,128)(2,1)} %copy-done.12) | copy-start | bytes 98308
  582.4 14.1 %all-to-all-start = ((bf16[2,32,1,960]{3,0,2,1:T(2,128)(2,1)}), bf16[2,32,1,960]{3,0,2,1:T(2,128)(2,1)S(1)}, u32[]{:S(2)}, u32[]{:S(2)}) async-start(bf16[2,32,1,960]{3,0,2,1:T(2,128)(2,1)} %pad_maximum_fusion.11), calls=%async_computation | async-start | bytes 262144 | tf_op jit(solution)/shard_map/all_to_all | solution.py:153
  589.1 300.5 %all-reduce.3.cloned.1.call-start = ((), (), s32[]{:S(2)}) async-start(), calls=%async_computation.6 | async-start | bytes 1048576
  596.5 357.8 %copy-start.1 = (bf16[2,8,5120]{2,1,0:T(8,128)(2,1)S(1)}, bf16[2,8,5120]{2,1,0:T(8,128)(2,1)}, u32[]{:S(2)}) copy-start(bf16[2,8,5120]{2,1,0:T(8,128)(2,1)} %param.16) | copy-start | bytes 491524
  600.1 1.6 copy-start.17
  601.6 343.4 %reduce-scatter.4.cloned.1.call-start = ((), (), s32[]{:S(2)}) async-start(), calls=%async_computation.5 | async-start | bytes 1310720
Sparse Core Ops, SparseCore 0:
  9.0 145.1 all-gather.5
  155.8 162.7 all-gather.3
  320.2 162.8 all-gather.7
  601.8 287.7 all-reduce.2
  892.0 53.0 reduce-scatter.3
where the time goes:
time: 962 us; the launch traced here: 961 us
  waiting for transfers between devices  747 us (78%)
  matrix products  72.7 us (8%)
  local copies, waits for them, and re-layouts  54.7 us (6%)
  blocking collectives  41.9 us (4%)
  other arithmetic  24.1 us (3%)
  between operations  14.1 us (1%)
    unnamed x7, waiting for transfers between devices  342 us
    all_gather x1, waiting for transfers between devices, body(): lax.all_gather(key_projection_matrix, 'dp', axis=0, tiled=True)  145 us
    all_gather x1, waiting for transfers between devices, body(): lax.all_gather(value_projection_matrix, 'dp', axis=0, tiled=True)  138 us
    all_gather x1, waiting for transfers between devices, body(): lax.all_gather(query_projection_matrix, 'dp', axis=0, tiled=True)  117 us
    dot_general x3, matrix products, add_rows(): jnp.dot(token_matrix, weight_piece, preferred_element_type=jnp.float32)  39.3 us
    psum x1, blocking collectives, body(): adapter_branch = lax.psum(branch_portion, 'tensor').astype(jnp.bfloat16)  34.5 us
    unnamed x32, local copies, waits for them, and re-layouts  21.5 us
  transfers between devices with their start and end apart: 6, of which 6 were waited for; matrix products, arithmetic and copies ran while one was open for 8% of the time, Pallas kernels for 0%

commit v1 on v0

--- a/solution.py
+++ b/solution.py
@@ -85,7 +85,12 @@
     def add_rows(weight_piece):
         return jnp.dot(token_matrix, weight_piece, preferred_element_type=jnp.float32)
 
-    plain_query = add_rows(lax.all_gather(query_projection_matrix, "dp", axis=0, tiled=True))
+    plain_query = add_rows(
+        jnp.concatenate(
+            lax.all_to_all(jnp.stack([query_projection_matrix] * lax.axis_size("dp")), "dp", 0, 0),
+            axis=0,
+        )
+    )
     base_key = add_rows(lax.all_gather(key_projection_matrix, "dp", axis=0, tiled=True))
     plain_value = add_rows(lax.all_gather(value_projection_matrix, "dp", axis=0, tiled=True))
     rotary_cosines, rotary_sines = rope_tables(seq_len, HEAD_DIM)

time: 962 us -> 874 us (0.909)
  waiting for transfers between devices: 747 us -> 651 us
    all_gather x1 -> x0, waiting for transfers between devices: 117 us -> none  [body(): lax.all_gather(query_projection_matrix, 'dp', axis=0, tiled=True)]
    all_to_all x0 -> x1, waiting for transfers between devices: none -> 78.6 us  [body(): lax.all_to_all(jnp.stack([query_projection_matrix] * lax.axis_size('dp'))...]
    all_gather x1, waiting for transfers between devices: 145 us -> 90 us  [body(): lax.all_gather(key_projection_matrix, 'dp', axis=0, tiled=True)]
    unnamed x7 -> x6, waiting for transfers between devices: 342 us -> 341 us
  transfers between devices with their start and end apart: 6 -> 6, of which waited for: 6 -> 6; matrix products, arithmetic and copies ran while one was open for 8% -> 9% of each run, Pallas kernels for 0% -> 0%
where the time goes in v1:
time: 874 us; the launch traced here: 872 us
  waiting for transfers between devices  651 us (74%)
  matrix products  73.6 us (8%)
  local copies, waits for them, and re-layouts  56.5 us (6%)
  blocking collectives  41.9 us (5%)
  other arithmetic  18.6 us (2%)
  starting transfers between devices  16.2 us (2%)
  between operations  14 us (2%)
    unnamed x6, waiting for transfers between devices  341 us
    all_gather x1, waiting for transfers between devices, body(): lax.all_gather(value_projection_matrix, 'dp', axis=0, tiled=True)  137 us
    all_gather x1, waiting for transfers between devices, body(): lax.all_gather(key_projection_matrix, 'dp', axis=0, tiled=True)  90 us
    all_to_all x1, waiting for transfers between devices, body(): lax.all_to_all(jnp.stack([query_projection_matrix] * lax.axis_size('dp'))...  78.6 us
    dot_general x3, matrix products, add_rows(): jnp.dot(token_matrix, weight_piece, preferred_element_type=jnp.float32)  40.3 us
    psum x1, blocking collectives, body(): adapter_branch = lax.psum(branch_portion, 'tensor').astype(jnp.bfloat16)  34.5 us
    unnamed x32, local copies, waits for them, and re-layouts  19 us
  transfers between devices with their start and end apart: 6, of which 6 were waited for; matrix products, arithmetic and copies ran while one was open for 9% of the time, Pallas kernels for 0%

profile of v1, /device:TPU:1, one launch (start us, length us, event | category | flops | bytes accessed | tf_op | source)
XLA Modules:
  0.0 872.2 jit_solution(1019238752235554070)
XLA Ops:
  6.5 0.7 all-gather.3.cloned.1.call-update
  7.3 0.7 all-gather.5.cloned.1.call-update
  8.0 4.1 stack.4
  12.1 9.5 %all-to-all-start = ((bf16[32,160,640]{2,1,0:T(8,128)(2,1)}), bf16[32,160,640]{2,1,0:T(8,128)(2,1)}, u32[]{:S(2)}, u32[]{:S(2)}) async-start(bf16[32,160,640]{2,1,0:T(8,128)(2,1)} %stack.4), calls=%async_computation | async-start | bytes 13107200 | tf_op jit(solution)/shard_map/all_to_all | solution.py:90
  21.6 0.7 copy.57
  22.3 13.8 %copy.51 = bf16[2,512,5120]{1,2,0:T(8,128)(2,1)} copy(bf16[2,512,5120]{2,1,0:T(8,128)(2,1)} %param.12) | data formatting | bytes 20971520 | tf_op args[0]
  36.0 0.5 fusion.70
  36.7 1.1 broadcast_select_fusion
  37.9 6.8 convolution_convert_fusion
  44.7 0.6 copy-done.12
  45.3 3.2 convolution_bitcast_fusion
  48.5 78.6 %all-to-all-done = bf16[32,160,640]{2,1,0:T(8,128)(2,1)} async-done(((bf16[32,160,640]{2,1,0:T(8,128)(2,1)}), bf16[32,160,640]{2,1,0:T(8,128)(2,1)}, u32[]{:S(2)}, u32[]{:S(2)}) %all-to-all-start) | async-done | bytes 6553632 | tf_op jit(solution)/shard_map/all_to_all | solution.py:90
  127.1 13.4 %fusion.46 = f32[1024,640]{1,0:T(8,128)S(1)} fusion(f32[1024,2,640]{2,0,1:T(8,128)} %convolution_bitcast_fusion, bf16[1024,5120]{1,0:T(8,128)(2,1)} %bitcast.137, bf16[5120,640]{1,0:T(8,128)(2,1)} %bitcast.19), kind=kOutput, calls=%fused_computation.52 | convolution fusion | flops 6712197120 | bytes 22282240 | tf_op jit(solution)/shard_map/dot_general | solution.py:86
  140.5 2.3 reshape.170
  142.8 3.3 copy.54
  146.2 90.0 %all-gather.3.cloned.1.call-done = bf16[5120,640]{1,0:T(8,128)(2,1)} async-done(((bf16[160,640]{1,0:T(8,128)(2,1)}), bf16[5120,640]{1,0:T(8,128)(2,1)}) %all-gather.3.cloned.1.call-update) | async-done | bytes 6553616 | tf_op jit(solution)/shard_map/all_gather | solution.py:94
  236.2 9.5 %copy.52 = bf16[640,5120]{1,0:T(8,128)(2,1)} copy(bf16[640,5120]{0,1:T(8,128)(2,1)} %bitcast.140) | data formatting | bytes 13107200 | tf_op jit(solution)/shard_map/dot_general | solution.py:86
  245.7 12.8 %fusion.39 = f32[2,512,5,128]{1,3,2,0:T(8,128)} fusion(bf16[5,128,5120,1]{2,1,0,3:T(8,128)(2,1)} %bitcast.141, bf16[2,512,5120]{2,1,0:T(8,128)(2,1)} %param.12), kind=kOutput, calls=%fused_computation.42 | convolution fusion | flops 6710886400 | bytes 19660800 | tf_op jit(solution)/shard_map/dot_general | solution.py:86
  258.5 137.5 %all-gather.5.cloned.1.call-done = bf16[5120,640]{1,0:T(8,128)(2,1)} async-done(((bf16[160,640]{1,0:T(8,128)(2,1)}), bf16[5120,640]{1,0:T(8,128)(2,1)}) %all-gather.5.cloned.1.call-update) | async-done | bytes 6553616 | tf_op jit(solution)/shard_map/all_gather | solution.py:95
  395.9 14.1 %fusion.44 = bf16[1024,640]{1,0:T(8,128)(2,1)} fusion(f32[1024,2,640]{2,0,1:T(8,128)} %convolution_bitcast_fusion, bf16[1024,5120]{1,0:T(8,128)(2,1)} %bitcast.138, bf16[5120,640]{1,0:T(8,128)(2,1)} %all-gather.5.cloned.1.call-done), kind=kOutput, calls=%fused_computation.49 | convolution fusion | flops 6712852480 | bytes 20971520 | tf_op jit(solution)/shard_map/dot_general | solution.py:86
  410.1 4.1 reshape.166
  414.1 3.1 copy.62
  417.2 0.8 slice_negate_fusion.1
  418.1 3.0 fusion.50
  421.0 22.2 %while.12 = (s32[]{:T(128)}, f32[2,512,5,128]{1,3,2,0:T(8,128)}, bf16[2,512,5,128]{1,3,2,0:T(8,128)(2,1)}, bf16[2,512,5,128]{1,3,2,0:T(8,128)(2,1)}, s32[2]{0:T(...) while((s32[]{:T(128)}, f32[2,512,5,128]{1,3,2,0:T(8,128)}, ...), condition=%wide.region_4.5_spmd, body=%wide.region_0.4_spmd.sunk | while | flops 1362688512 | bytes 75326712 | solution.py:121
  421.0 2.2 fusion.110
  423.2 0.6 dynamic_slice.73
  423.8 0.6 iota_compare_fusion.4
  424.6 2.5 fusion.112
  427.2 1.0 fusion.114
  428.5 0.9 multiply_reduce_fusion.2
  429.4 0.6 copy-done.2
  430.0 2.2 fusion.113
  432.2 2.2 fusion.110
  434.3 0.6 dynamic_slice.73
  434.9 0.6 iota_compare_fusion.4
  435.7 2.5 fusion.112
  438.3 1.0 fusion.114
  439.6 0.8 multiply_reduce_fusion.2
  440.5 0.6 copy-done.2
  441.1 2.2 fusion.113
  443.3 2.1 broadcast_multiply_fusion
  445.7 2.5 fusion.51
  448.2 1.7 copy.63
  449.9 1.4 copy.64
  451.3 2.1 fusion.67
  453.4 34.5 %psum.14 = bf16[2,512,2,8]{1,3,2,0:T(8,128)(2,1)S(1)} all-reduce(f32[2,512,2,8]{1,3,2,0:T(8,128)S(1)} %fusion.67), channel_id=1, replica_groups=mesh['dp'=32,'tensor'=4] {'tensor'}, use_global_device_ids=true, to_apply=%region_5.6 | all-reduce | flops 16384 | bytes 98304 | tf_op jit(solution)/shard_map/psum | solution.py:134
  487.9 3.3 fusion.63
  491.6 0.5 fusion.68
  492.4 0.4 copy.67
  492.9 0.8 pad_maximum_fusion.11
  493.7 6.6 all-to-all-start.1
  500.4 3.5 reshape.159
  504.0 3.8 all-to-all-done.1
  507.9 3.6 fusion.71
  511.5 1.5 fusion.41
  513.0 0.6 dynamic-slice
  514.3 286.6 %all-reduce.3.cloned.1.call-done = bf16[64,4096]{1,0:T(8,128)(2,1)} async-done(((bf16[64,4096]{1,0:T(8,128)(2,1)}), bf16[64,4096]{1,0:T(8,128)(2,1)}) %all-reduce.3.cloned.1.call-update) | async-done | bytes 524304
  800.9 0.9 constant_dynamic-slice_fusion
  801.7 1.4 copy.79
  803.1 53.3 %reduce-scatter.4.cloned.1.call-done = bf16[1024,2]{1,0:T(8,128)(2,1)} async-done(((bf16[4096,2]{1,0:T(8,128)(2,1)}), bf16[1024,2]{1,0:T(8,128)(2,1)}) %reduce-scatter.4.cloned.1.call-update) | async-done | bytes 4112
  856.4 1.1 copy.80
  857.6 7.4 psum.15
  865.0 0.7 convert_multiply_fusion
  (64 shorter events, 2.6 us)
Async XLA Ops:
  6.5 31.3 %copy-start = (bf16[2,8,5120]{2,1,0:T(8,128)(2,1)S(1)}, bf16[2,8,5120]{2,1,0:T(8,128)(2,1)}, u32[]{:S(2)}) copy-start(bf16[2,8,5120]{2,1,0:T(8,128)(2,1)} %param.16) | copy-start | bytes 491524
  6.5 229.6 %all-gather.3.cloned.1.call-start = ((), (), s32[]{:S(2)}) async-start(), calls=%async_computation.3 | async-start | bytes 6758400 | tf_op jit(solution)/shard_map/all_gather | solution.py:94
  7.3 388.7 %all-gather.5.cloned.1.call-start = ((), (), s32[]{:S(2)}) async-start(), calls=%async_computation.4 | async-start | bytes 6758400 | tf_op jit(solution)/shard_map/all_gather | solution.py:95
  12.1 9.5 %copy-start.4 = (bf16[2,512,640]{2,1,0:T(8,128)(2,1)S(1)}, bf16[2,512,640]{2,1,0:T(8,128)(2,1)}, u32[]{:S(2)}) copy-start(bf16[2,512,640]{2,1,0:T(8,128)(2,1)} %param.18) | copy-start | bytes 3932164
  12.1 115.0 %all-to-all-start = ((bf16[32,160,640]{2,1,0:T(8,128)(2,1)}), bf16[32,160,640]{2,1,0:T(8,128)(2,1)}, u32[]{:S(2)}, u32[]{:S(2)}) async-start(bf16[32,160,640]{2,1,0:T(8,128)(2,1)} %stack.4), calls=%async_computation | async-start | bytes 13107200 | tf_op jit(solution)/shard_map/all_to_all | solution.py:90
  22.3 14.4 %copy-start.16 = (s32[2]{0:T(128)S(1)}, s32[2]{0:T(128)}, u32[]{:S(2)}) copy-start(s32[2]{0:T(128)} %param.19) | copy-start | bytes 28
  37.9 7.4 copy-start.14
  44.7 0.6 copy-start.12
  414.1 3.1 copy-start.3
  424.6 2.6 copy-start.5
  424.6 2.6 copy-start.11
  427.2 1.3 copy-start.8
  428.2 1.2 copy-start.6
  428.5 1.5 copy-start.2
  435.7 2.6 copy-start.5
  435.7 2.6 copy-start.11
  438.3 1.3 copy-start.8
  439.3 1.2 copy-start.6
  439.6 1.5 copy-start.2
  448.1 1.7 copy-start.7
  448.1 3.2 copy-start.15
  449.9 1.4 copy-start.9
  453.4 38.1 %copy-start.10 = (bf16[2,512,1,640]{3,1,2,0:T(8,128)(2,1)S(1)}, bf16[2,512,1,640]{3,1,2,0:T(8,128)(2,1)}, u32[]{:S(2)}) copy-start(bf16[2,512,1,640]{3,1,2,0:T(8,128)(2,1)} %copy.64) | copy-start | bytes 3932164
  453.4 38.1 %copy-start.13 = (bf16[1024,2,8]{0,2,1:T(8,128)(2,1)S(1)}, bf16[1024,2,8]{0,2,1:T(8,128)(2,1)}, u32[]{:S(2)}) copy-start(bf16[1024,2,8]{0,2,1:T(8,128)(2,1)} %copy-done.12) | copy-start | bytes 98308
  493.7 14.1 %all-to-all-start.1 = ((bf16[2,32,1,960]{3,0,2,1:T(2,128)(2,1)}), bf16[2,32,1,960]{3,0,2,1:T(2,128)(2,1)S(1)}, u32[]{:S(2)}, u32[]{:S(2)}) async-start(bf16[2,32,1,960]{3,0,2,1:T(2,128)(2,1)} %pad_maximum_fusion.11), calls=%async_computation.1 | async-start | bytes 262144 | tf_op jit(solution)/shard_map/all_to_all | solution.py:158
  500.4 300.5 %all-reduce.3.cloned.1.call-start = ((), (), s32[]{:S(2)}) async-start(), calls=%async_computation.6 | async-start | bytes 1048576
  507.9 357.8 %copy-start.1 = (bf16[2,8,5120]{2,1,0:T(8,128)(2,1)S(1)}, bf16[2,8,5120]{2,1,0:T(8,128)(2,1)}, u32[]{:S(2)}) copy-start(bf16[2,8,5120]{2,1,0:T(8,128)(2,1)} %param.16) | copy-start | bytes 491524
  511.5 1.6 copy-start.17
  513.0 343.4 %reduce-scatter.4.cloned.1.call-start = ((), (), s32[]{:S(2)}) async-start(), calls=%async_computation.5 | async-start | bytes 1310720
Sparse Core Ops, SparseCore 0:
  9.0 227.1 all-gather.2
  237.8 158.0 all-gather.4
  513.1 287.7 all-reduce.2
  803.3 53.0 reduce-scatter.3
